TPU v7x, 128 devices: a whole 4x4x4 slice. The times are simulated.
128 devices in a mesh: lon: 16 (over y_hi, x, core), lat: 8 (over y_lo, z).
Axes of the slice: x: 4, y: 4 (y_hi: 2, y_lo: 2; y = y_hi * 2 + y_lo), z: 4, core: 2. Of those that a mesh axis runs over, the one named last changes fastest.
Arguments:
- grid_state: bfloat16 [1024, 256, 384], P('lon', 'lat'), may hold values from -6 to 6
- conv_weight: bfloat16 [9, 384, 384], replicated, may hold values from -0.109375 to 0.109375
- mix_weight: bfloat16 [384, 384], replicated, may hold values from -0.3125 to 0.3125
- teacher: bfloat16 [8, 128, 256, 384], P('lat', 'lon'), may hold values from -6 to 6
- tile_mask: int32 [16, 8, 8], P('lon', 'lat'), may hold values from 0 to 1, as said below
- source_owner: int32 [8, 16, 16], P('lat'), may hold values from 0 to 15, as said below
- source_block: int32 [8, 16, 16], P('lat'), may hold values from 0 to 7
- margin_weight: float32 [8, 16, 16], P('lat', 'lon'), may hold values from 0.2 to 1
Outputs:
- next_state: bfloat16 [1024, 256, 384], P('lon', 'lat')
- misfit: bfloat16 [1024, 256, 384], P('lon', 'lat')
- grad_conv: float32 [9, 384, 384], replicated
- grad_mix: float32 [384, 384], replicated
Inputs may be any that keep to these rules, and one draw needn't show every extreme that they name: `tile_mask`: 1 marks an ocean tile; every device holds 1 to 4 ocean tiles, and some device holds exactly 4. `source_owner`: blocks lie in the tile's own latitude row. Among the 16 entries of one device no lon index appears more than 2 times, and on every device some lon index appears exactly 2 times.
All inputs are finite; a program needn't handle non-finite values.
Results may differ from a plain program's by a relative error of at most 0.0032.
Values may be sent and summed in bfloat16 or wider, within the bound.
A program may use at most 128 MiB of HBM per device.

v0:
```python
import math
import jax
import jax.numpy as jnp
from jax import lax
from jax.sharding import PartitionSpec as P

TS = 16
K = 2


def with_halo(cells, sides, width, closed):
    for axis, dim in sides:
        count = lax.axis_size(axis)
        ends = count if closed else count - 1
        head = lax.slice_in_dim(cells, 0, width, axis=dim)
        tail = lax.slice_in_dim(cells, cells.shape[dim] - width, cells.shape[dim], axis=dim)
        cells = jnp.concatenate(
            [
                lax.ppermute(tail, axis, [(i, (i + 1) % count) for i in range(ends)]),
                cells,
                lax.ppermute(head, axis, [((i + 1) % count, i) for i in range(ends)]),
            ],
            axis=dim,
        )
    return cells


def block_step(windows, centre, target, keep_rows, conv_weight, mix_weight, scale):
    count, height, breadth, chans = windows.shape
    height = height - 2
    breadth = breadth - 2
    row_count = count * height * breadth

    def shifted(offset):
        step_lon, step_lat = divmod(offset, 3)
        return windows[:, step_lon : step_lon + height, step_lat : step_lat + breadth, :].reshape(
            row_count, chans
        )

    pre = jnp.zeros((row_count, chans), jnp.float32)
    for offset in range(9):
        pre = pre + jnp.dot(
            shifted(offset), conv_weight[offset], preferred_element_type=jnp.float32
        )
    sigmoid_pre = jax.nn.sigmoid(pre)
    hidden = (pre * sigmoid_pre).astype(jnp.bfloat16)
    full_state = centre.astype(jnp.float32) + jnp.dot(
        hidden, mix_weight, preferred_element_type=jnp.float32
    )
    next_state = (keep_rows * full_state).astype(jnp.bfloat16)
    error = keep_rows * (full_state - target)
    misfit = error.astype(jnp.bfloat16)
    scaled = (error * scale).astype(jnp.bfloat16)
    grad_mix = lax.dot_general(
        hidden, scaled, (((0,), (0,)), ((), ())), preferred_element_type=jnp.float32
    )
    back_grad = lax.dot_general(
        scaled, mix_weight, (((1,), (1,)), ((), ())), preferred_element_type=jnp.float32
    )
    dpre = (back_grad * sigmoid_pre * (1.0 + pre * (1.0 - sigmoid_pre))).astype(jnp.bfloat16)
    grad_conv = jnp.stack(
        [
            lax.dot_general(
                shifted(offset), dpre, (((0,), (0,)), ((), ())), preferred_element_type=jnp.float32
            )
            for offset in range(9)
        ]
    )
    return (next_state, misfit, grad_conv, grad_mix)


def tiles_to_block(tiles, tiles_lon, tiles_lat, side):
    chans = tiles.shape[-1]
    shaped = tiles.reshape(tiles_lon, tiles_lat, side, side, chans)
    return jnp.transpose(shaped, (0, 2, 1, 3, 4)).reshape(tiles_lon * side, tiles_lat * side, chans)


def body(
    grid_state,
    conv_weight,
    mix_weight,
    teacher,
    tile_mask,
    source_owner,
    source_block,
    margin_weight,
):
    lon_count = lax.axis_size("lon")
    lat_count = lax.axis_size("lat")
    my_lon = lax.axis_index("lon")
    width_lon, width_lat, chans = grid_state.shape
    side = TS
    tiles_lon = width_lon // side
    tiles_lat = width_lat // side
    tile_count = tiles_lon * tiles_lat
    cells_tile = side * side
    owners = source_owner[0]
    blocks = source_block[0]
    my_owner = lax.dynamic_index_in_dim(owners, my_lon, 0, keepdims=False)
    my_block = lax.dynamic_index_in_dim(blocks, my_lon, 0, keepdims=False)
    local_blocks = teacher[0]
    held = local_blocks.shape[0]
    wanted = my_owner * held + my_block
    piece = lax.all_gather(local_blocks, "lon", axis=0, tiled=True)
    rows_here = jnp.arange(piece.shape[0], dtype=jnp.int32)
    pick_rows = (wanted[:, None] == rows_here[None, :]).astype(jnp.bfloat16)
    picked = jnp.einsum("rj,jcx->rcx", pick_rows, piece, preferred_element_type=jnp.float32)
    weights = margin_weight[0, 0]
    mixed = picked * weights[:, None, None]
    target_tiles = jnp.sum(mixed.reshape(tile_count, K, cells_tile, chans), axis=1)
    lon_wide = with_halo(grid_state, (("lon", 0),), 1, True)
    padded = with_halo(lon_wide, (("lat", 1),), 1, False)
    scale = 1.0 / math.sqrt(width_lon * lon_count * width_lat * lat_count)
    ocean_tiles = tile_mask[0, 0]
    ocean_grid = ocean_tiles.astype(jnp.float32).reshape(tiles_lon, tiles_lat)
    keep_rows = jnp.broadcast_to(
        ocean_grid[:, None, :, None], (tiles_lon, side, tiles_lat, side)
    ).reshape(width_lon * width_lat, 1)
    target_rows = tiles_to_block(target_tiles, tiles_lon, tiles_lat, side).reshape(
        width_lon * width_lat, chans
    )
    next_rows, misfit_rows, grad_conv, grad_mix = block_step(
        padded[None],
        grid_state.reshape(width_lon * width_lat, chans),
        target_rows,
        keep_rows,
        conv_weight,
        mix_weight,
        scale,
    )
    next_state = next_rows.reshape(width_lon, width_lat, chans)
    misfit = misfit_rows.reshape(width_lon, width_lat, chans)
    grad_conv, grad_mix = lax.psum((grad_conv, grad_mix), ("lon", "lat"))
    return (next_state, misfit, grad_conv, grad_mix)


def solution(mesh):
    in_specs = (
        P("lon", "lat", None),
        P(),
        P(),
        P("lat", "lon", None, None),
        P("lon", "lat", None),
        P("lat", None, None),
        P("lat", None, None),
        P("lat", "lon", None),
    )
    out_specs = (P("lon", "lat", None), P("lon", "lat", None), P(), P())
    return jax.shard_map(body, mesh=mesh, in_specs=in_specs, out_specs=out_specs, check_vma=False)
```

profile of v0, /device:TPU:1, one launch (start us, length us, event | category | flops | bytes accessed | tf_op | source)
XLA Modules:
  0.0 406.9 jit_solution(4890446071105545086)
XLA Ops:
  7.2 3.6 copy.15
  11.5 1.4 collective-permute-start.1
  13.0 1.2 collective-permute-start
  14.2 4.4 %collective-permute-done = bf16[1,32,384]{2,1,0:T(8,128)(2,1)S(1)} collective-permute-done((bf16[1,32,384]{2,1,0:T(8,128)(2,1)S(1)}, bf16[1,32,384]{2,1,0:T(8,128)(2,1)S(1)}, u32[]{:S(2)}, u32[]{:S(2)}) %collective-permute-start) | collective-permute-done | bytes 24608 | tf_op jit(solution)/shard_map/ppermute | solution.py:19
  19.1 3.5 collective-permute-start.2
  22.6 1.3 collective-permute-start.3
  25.0 3.2 collective-permute-done.3
  28.2 1.3 maximum_bitcast_fusion
  29.5 4.9 %fusion.48 = (bf16[1,64,32,384]{3,2,1,0:T(8,128)(2,1)}, bf16[1,64,32,384]{3,2,1,0:T(8,128)(2,1)S(1)}, bf16[1,64,32,384]{3,2,1,0:T(8,128)(2,1)S(1)}, bf16[1,64,32...) fusion(bf16[1,66,34,384]{3,2,1,0:T(8,128)(2,1)S(1)} %maximum_bi, ...), kind=kLoop, calls=%fused_computation.69 | loop fusion | bytes 28311552 | tf_op jit(solution)/shard_map/slice | solution.py:36
  34.5 2.5 fusion.16
  37.0 1.5 copy-done.19
  40.7 1.1 fusion.22
  46.6 4.9 %add_add_fusion = f32[2048,384]{1,0:T(8,128)} fusion(f32[2048,384]{1,0:T(8,128)S(1)} %fusion.16, f32[2048,384]{1,0:T(8,128)S(1)} %fusion.18, f32[2048,384]{1,0:T(8,128)S(1)} %fusion.20, f32[2048,384]{1,0:T(8,128)S(1)} %fusion.22, f32[2048,384]{1,0:T(8,128)S(1)} %fusion.24, f32[2048,384]{1,0:T(8,128)S(1)} %fusion.26, f32[2048,384]{1,0:T(8,128)S(1)} %fusion.30, ...), kind=kOutput, calls=%fused_computation.11 | convolution fusion | flops 610271232 | bytes 30179328 | tf_op jit(solution)/shard_map/dot_general | solution.py:42
  51.5 129.9 %all-gather.3.cloned.1.call-done = bf16[1,128,256,384]{3,1,2,0:T(8,128)(2,1)} async-done(((bf16[1,8,256,384]{3,1,2,0:T(8,128)(2,1)}), bf16[1,128,256,384]{3,1,2,0:T(8,128)(2,1)}) %all-gather.3.cloned.1.call-update) | async-done | bytes 25165840 | tf_op jit(solution)/shard_map/all_gather | solution.py:104
  181.4 12.9 %broadcast_multiply_fusion = f32[16,256,384]{2,0,1:T(8,128)} fusion(f32[16]{0:T(128)S(1)} %bitcast.148, bf16[1,128,256,384]{3,1,2,0:T(8,128)(2,1)} %all-gather.3.cloned.1.call-done, s32[16]{0:T(128)S(1)} %add_bitcast_fusion), kind=kOutput, calls=%fused_computation.7 | convolution fusion | flops 404228096 | bytes 31457408 | tf_op jit(solution)/shard_map/rj,jcx->rcx/dot_general | solution.py:107
  194.3 8.2 %reshape.95 = f32[8,2,256,384]{3,1,0,2:T(2,128)} reshape(f32[16,256,384]{2,0,1:T(8,128)} %broadcast_multiply_fusion) | data formatting | bytes 12582912 | tf_op jit(solution)/shard_map/reshape | solution.py:110
  202.5 10.3 %reduce_sum.9 = f32[8,256,384]{2,0,1:T(8,128)S(1)} reduce(f32[8,2,256,384]{3,1,0,2:T(2,128)} %reshape.95, f32[]{:T(128)} %constant.22.clone.1), dimensions={1}, to_apply=%region_0.1 | reduce | flops 786432 | bytes 9437188 | tf_op jit(solution)/shard_map/reduce_sum | solution.py:110
  213.8 1.4 copy-done.18
  215.7 3.2 fusion.46
  218.9 1.9 fusion.14
  220.8 1.8 multiply_convert_fusion
  222.6 1.8 fusion.13
  224.4 1.8 fusion.12
  226.2 1.8 fusion.11
  228.1 1.8 fusion.10
  229.9 1.8 fusion.9
  231.8 1.8 fusion.8
  233.6 1.8 fusion.7
  235.4 1.8 fusion.6
  237.2 1.8 fusion.5
  239.1 154.6 %all-reduce.3.cloned.1.call-done = (f32[9,384,384]{2,1,0:T(8,128)}, f32[384,384]{1,0:T(8,128)}) async-done(((f32[9,384,384]{2,1,0:T(8,128)}, f32[384,384]{1,0:T(8,128)}), (f32[9,384,384]{2,1,0:T(8,128)}, f32[384,384]{1,0:T(8,128)})) %all-reduce.3.cloned.1.call-update) | async-done | bytes 5898256 | tf_op jit(solution)/shard_map/psum | solution.py:133
  393.7 5.3 %copy.30 = f32[9,384,384]{2,1,0:T(8,128)} copy(f32[9,384,384]{2,1,0:T(8,128)} %get-tuple-element.24) | data formatting | bytes 10616832
  (73 shorter events, 11.6 us)
Async XLA Ops:
  7.2 206.7 %copy-start = (bf16[384,384]{1,0:T(8,128)(2,1)S(1)}, bf16[384,384]{1,0:T(8,128)(2,1)}, u32[]{:S(2)}) copy-start(bf16[384,384]{1,0:T(8,128)(2,1)} %param.10) | copy-start | bytes 884740
  7.2 3.7 copy-start.20
  7.2 7.0 %copy-start.24 = (s32[1,1,8]{2,1,0:T(1,128)S(1)}, s32[1,1,8]{2,1,0:T(1,128)}, u32[]{:S(2)}) copy-start(s32[1,1,8]{2,1,0:T(1,128)} %param.12) | copy-start | bytes 100
  7.2 174.2 %all-gather.3.cloned.1.call-start = ((), (), s32[]{:S(2)}) async-start(), calls=%async_computation | async-start | bytes 26738688 | tf_op jit(solution)/shard_map/all_gather | solution.py:104
  10.9 382.8 %all-reduce.3.cloned.1.call-start = ((), (), s32[]{:S(2)}) async-start(), calls=%async_computation.1 | async-start | bytes 11796480 | tf_op jit(solution)/shard_map/psum | solution.py:133
  11.5 7.3 %collective-permute-start.1 = (bf16[1,32,384]{2,1,0:T(8,128)(2,1)}, bf16[1,32,384]{2,1,0:T(8,128)(2,1)S(1)}, u32[]{:S(2)}, u32[]{:S(2)}) collective-permute-start(bf16[1,32,384]{2,1,0:T(8,128)(2,1)} %get-tuple-element.20), channel_id=1, source_target_pairs={{8,0},{16,8},{24,16},{32,24},{40,32},{48,40},{56,48},{64,56},{72,6... | collective-permute-start | bytes 73736 | tf_op jit(solution)/shard_map/ppermute | solution.py:21
  13.0 5.6 %collective-permute-start = (bf16[1,32,384]{2,1,0:T(8,128)(2,1)S(1)}, bf16[1,32,384]{2,1,0:T(8,128)(2,1)S(1)}, u32[]{:S(2)}, u32[]{:S(2)}) collective-permute-start(bf16[1,32,384]{2,1,0:T(8,128)(2,1)S(1)} %get-tuple-element.21), channel_id=1, source_target_pairs={{0,8},{8,16},{16,24},{24,32},{32,40},{40,48},{48,56},{56,64},{64,7... | collective-permute-start | bytes 73736 | tf_op jit(solution)/shard_map/ppermute | solution.py:19
  19.1 5.9 %collective-permute-start.2 = (bf16[66,1,384]{2,1,0:T(2,128)(2,1)S(1)}, bf16[66,1,384]{2,1,0:T(2,128)(2,1)S(1)}, u32[]{:S(2)}, u32[]{:S(2)}) collective-permute-start(bf16[66,1,384]{2,1,0:T(2,128)(2,1)S(1)} %get-tuple-element.18), channel_id=1, source_target_pairs={{0,1},{1,2},{2,3},{3,4},{4,5},{5,6},{6,7},{8,9},{9,10},{10,11},{11... | collective-permute-start | bytes 152072 | tf_op jit(solution)/shard_map/ppermute | solution.py:19
  22.6 5.6 %collective-permute-start.3 = (bf16[66,1,384]{2,1,0:T(2,128)(2,1)S(1)}, bf16[66,1,384]{2,1,0:T(2,128)(2,1)S(1)}, u32[]{:S(2)}, u32[]{:S(2)}) collective-permute-start(bf16[66,1,384]{2,1,0:T(2,128)(2,1)S(1)} %get-tuple-element.19), channel_id=1, source_target_pairs={{1,0},{2,1},{3,2},{4,3},{5,4},{6,5},{7,6},{9,8},{10,9},{11,10},{12... | collective-permute-start | bytes 152072 | tf_op jit(solution)/shard_map/ppermute | solution.py:21
  34.4 2.6 copy-start.1
  34.4 2.6 copy-start.3
  34.4 5.2 %copy-start.5 = (bf16[1,64,32,384]{3,2,1,0:T(8,128)(2,1)}, bf16[1,64,32,384]{3,2,1,0:T(8,128)(2,1)S(1)}, u32[]{:S(2)}) copy-start(bf16[1,64,32,384]{3,2,1,0:T(8,128)(2,1)S(1)} %get-tuple-element.12) | copy-start | bytes 4718596
  34.4 6.3 %copy-start.7 = (bf16[1,64,32,384]{3,2,1,0:T(8,128)(2,1)}, bf16[1,64,32,384]{3,2,1,0:T(8,128)(2,1)S(1)}, u32[]{:S(2)}) copy-start(bf16[1,64,32,384]{3,2,1,0:T(8,128)(2,1)S(1)} %get-tuple-element.13) | copy-start | bytes 4718596
  34.4 7.4 %copy-start.9 = (bf16[1,64,32,384]{3,2,1,0:T(8,128)(2,1)}, bf16[1,64,32,384]{3,2,1,0:T(8,128)(2,1)S(1)}, u32[]{:S(2)}) copy-start(bf16[1,64,32,384]{3,2,1,0:T(8,128)(2,1)S(1)} %get-tuple-element.14) | copy-start | bytes 4718596
  34.4 8.5 %copy-start.11 = (bf16[1,64,32,384]{3,2,1,0:T(8,128)(2,1)}, bf16[1,64,32,384]{3,2,1,0:T(8,128)(2,1)S(1)}, u32[]{:S(2)}) copy-start(bf16[1,64,32,384]{3,2,1,0:T(8,128)(2,1)S(1)} %get-tuple-element.15) | copy-start | bytes 4718596
  34.4 9.6 %copy-start.13 = (bf16[1,64,32,384]{3,2,1,0:T(8,128)(2,1)}, bf16[1,64,32,384]{3,2,1,0:T(8,128)(2,1)S(1)}, u32[]{:S(2)}) copy-start(bf16[1,64,32,384]{3,2,1,0:T(8,128)(2,1)S(1)} %get-tuple-element.16) | copy-start | bytes 4718596
  34.4 4.0 copy-start.19
  44.1 1.4 copy-start.15
  46.6 134.8 %copy-start.23 = (f32[1,1,16]{2,1,0:T(1,128)S(1)}, f32[1,1,16]{2,1,0:T(1,128)}, u32[]{:S(2)}) copy-start(f32[1,1,16]{2,1,0:T(1,128)} %param.15) | copy-start | bytes 196
  213.3 1.9 copy-start.18
  213.4 2.3 copy-start.21
  220.8 1.8 copy-start.16
  222.6 1.8 copy-start.14
  224.4 1.8 copy-start.12
  226.2 1.8 copy-start.10
  228.1 1.8 copy-start.8
  229.9 1.8 copy-start.6
  231.7 1.8 copy-start.4
  233.6 1.8 copy-start.2
  235.4 1.8 copy-start.17
  393.7 5.3 %copy-start.22 = (f32[384,384]{1,0:T(8,128)S(1)}, f32[384,384]{1,0:T(8,128)}, u32[]{:S(2)}) copy-start(f32[384,384]{1,0:T(8,128)} %get-tuple-element.25) | copy-start | bytes 1769476
Sparse Core Ops, SparseCore 0:
  11.0 170.3 all-gather.2
  239.2 154.4 all-reduce.2
where the time goes:
time: 412 us; the launch traced here: 407 us
  waiting for transfers between devices  292 us (71%)
  matrix products  51.3 us (12%)
  local copies, waits for them, and re-layouts  29 us (7%)
  between operations  14.6 us (4%)
  other arithmetic  12.3 us (3%)
  starting transfers between devices  7.52 us (2%)
    psum x1, waiting for transfers between devices, body(): grad_conv, grad_mix = lax.psum((grad_conv, grad_mix), ('lon', 'lat'))  155 us
    all_gather x1, waiting for transfers between devices, body(): piece = lax.all_gather(local_blocks, 'lon', axis=0, tiled=True)  130 us
    dot_general x9, matrix products, block_step(): lax.dot_general(shifted(offset), dpre, (((0,), (0,)), ((), ())), preferre...  16.4 us
    dot_general x9, matrix products, block_step(): jnp.dot(shifted(offset), conv_weight[offset], preferred_element_type=jnp....  15.1 us
    unnamed x55, local copies, waits for them, and re-layouts  13.8 us
    dot_general x1, matrix products, body(): jnp.einsum('rj,jcx->rcx', pick_rows, piece, preferred_element_type=jnp.fl...  12.9 us
    reduce_sum x1, other arithmetic, body(): jnp.sum(mixed.reshape(tile_count, K, cells_tile, chans), axis=1)  10.3 us
  transfers between devices with their start and end apart: 6, of which 4 were waited for; matrix products, arithmetic and copies ran while one was open for 6% of the time, Pallas kernels for 0%

commit v1 on v0

--- a/solution.py
+++ b/solution.py
@@ -130,7 +130,7 @@
     )
     next_state = next_rows.reshape(width_lon, width_lat, chans)
     misfit = misfit_rows.reshape(width_lon, width_lat, chans)
-    grad_conv, grad_mix = lax.psum((grad_conv, grad_mix), ("lon", "lat"))
+    grad_conv, grad_mix = lax.psum(lax.psum((grad_conv, grad_mix), "lon"), "lat")
     return (next_state, misfit, grad_conv, grad_mix)
 
 

time: 412 us -> 552 us (1.34)
  waiting for transfers between devices: 292 us -> 432 us
    psum x1 -> x2, waiting for transfers between devices: 155 us -> 295 us  [the longest x1 152 us: body(): lax.psum((grad_conv, grad_mix), 'lon')]
  transfers between devices with their start and end apart: 6 -> 7, of which waited for: 4 -> 5; matrix products, arithmetic and copies ran while one was open for 6% -> 4% of each run, Pallas kernels for 0% -> 0%
where the time goes in v1:
time: 552 us; the launch traced here: 547 us
  waiting for transfers between devices  432 us (78%)
  matrix products  51.3 us (9%)
  local copies, waits for them, and re-layouts  29 us (5%)
  between operations  14.3 us (3%)
  other arithmetic  12.3 us (2%)
  starting transfers between devices  7.56 us (1%)
    psum x1, waiting for transfers between devices, body(): lax.psum((grad_conv, grad_mix), 'lon')  152 us
    psum x1, waiting for transfers between devices, body(): lax.psum(lax.psum((grad_conv, grad_mix), 'lon'), 'lat')  142 us
    all_gather x1, waiting for transfers between devices, body(): piece = lax.all_gather(local_blocks, 'lon', axis=0, tiled=True)  130 us
    dot_general x9, matrix products, block_step(): lax.dot_general(shifted(offset), dpre, (((0,), (0,)), ((), ())), preferre...  16.4 us
    dot_general x9, matrix products, block_step(): jnp.dot(shifted(offset), conv_weight[offset], preferred_element_type=jnp....  15.1 us
    unnamed x55, local copies, waits for them, and re-layouts  13.8 us
    dot_general x1, matrix products, body(): jnp.einsum('rj,jcx->rcx', pick_rows, piece, preferred_element_type=jnp.fl...  12.9 us
  transfers between devices with their start and end apart: 7, of which 5 were waited for; matrix products, arithmetic and copies ran while one was open for 4% of the time, Pallas kernels for 0%

profile of v1, /device:TPU:1, one launch (start us, length us, event | category | flops | bytes accessed | tf_op | source)
XLA Modules:
  0.0 546.9 jit_solution(13987316191382114208)
XLA Ops:
  7.2 3.6 copy.15
  11.5 1.4 collective-permute-start.1
  13.0 1.2 collective-permute-start
  14.2 4.4 collective-permute-done
  19.1 3.5 collective-permute-start.2
  22.6 1.3 collective-permute-start.3
  25.0 3.2 collective-permute-done.3
  28.2 1.3 maximum_bitcast_fusion
  29.5 4.9 fusion.48
  34.5 2.5 fusion.16
  37.0 1.5 copy-done.19
  46.6 4.9 add_add_fusion
  51.5 129.9 %all-gather.3.cloned.1.call-done = bf16[1,128,256,384]{3,1,2,0:T(8,128)(2,1)} async-done(((bf16[1,8,256,384]{3,1,2,0:T(8,128)(2,1)}), bf16[1,128,256,384]{3,1,2,0:T(8,128)(2,1)}) %all-gather.3.cloned.1.call-update) | async-done | bytes 25165840 | tf_op jit(solution)/shard_map/all_gather | solution.py:104
  181.4 12.9 %broadcast_multiply_fusion = f32[16,256,384]{2,0,1:T(8,128)} fusion(f32[16]{0:T(128)S(1)} %bitcast.148, bf16[1,128,256,384]{3,1,2,0:T(8,128)(2,1)} %all-gather.3.cloned.1.call-done, s32[16]{0:T(128)S(1)} %add_bitcast_fusion), kind=kOutput, calls=%fused_computation.7 | convolution fusion | flops 404228096 | bytes 31457408 | tf_op jit(solution)/shard_map/rj,jcx->rcx/dot_general | solution.py:107
  194.3 8.2 %reshape.95 = f32[8,2,256,384]{3,1,0,2:T(2,128)} reshape(f32[16,256,384]{2,0,1:T(8,128)} %broadcast_multiply_fusion) | data formatting | bytes 12582912 | tf_op jit(solution)/shard_map/reshape | solution.py:110
  202.5 10.3 %reduce_sum.9 = f32[8,256,384]{2,0,1:T(8,128)S(1)} reduce(f32[8,2,256,384]{3,1,0,2:T(2,128)} %reshape.95, f32[]{:T(128)} %constant.22.clone.1), dimensions={1}, to_apply=%region_0.1 | reduce | flops 786432 | bytes 9437188 | tf_op jit(solution)/shard_map/reduce_sum | solution.py:110
  213.9 1.4 copy-done.18
  215.7 3.2 fusion.46
  218.9 1.9 fusion.14
  220.8 1.8 multiply_convert_fusion
  222.6 1.8 fusion.13
  224.4 1.8 fusion.12
  226.3 1.8 fusion.11
  228.1 1.8 fusion.10
  229.9 1.8 fusion.9
  231.8 1.8 fusion.8
  233.6 1.8 fusion.7
  235.4 1.8 fusion.6
  237.3 1.8 fusion.5
  239.2 152.5 %all-reduce.5.cloned.1.call-done = (f32[9,384,384]{2,1,0:T(8,128)}, f32[384,384]{1,0:T(8,128)}) async-done(((f32[9,384,384]{2,1,0:T(8,128)}, f32[384,384]{1,0:T(8,128)}), (f32[9,384,384]{2,1,0:T(8,128)}, f32[384,384]{1,0:T(8,128)})) %all-reduce.5.cloned.1.call-update) | async-done | bytes 5898256 | tf_op jit(solution)/shard_map/psum | solution.py:133
  391.7 142.4 %all-reduce.7.cloned.1.call-done = (f32[9,384,384]{2,1,0:T(8,128)}, f32[384,384]{1,0:T(8,128)}) async-done(((f32[9,384,384]{2,1,0:T(8,128)}, f32[384,384]{1,0:T(8,128)}), (f32[9,384,384]{2,1,0:T(8,128)}, f32[384,384]{1,0:T(8,128)})) %all-reduce.7.cloned.1.call-update) | async-done | bytes 5898256 | tf_op jit(solution)/shard_map/psum | solution.py:133
  534.1 5.3 copy.32
  (76 shorter events, 12.8 us)
Async XLA Ops:
  7.2 206.7 %copy-start = (bf16[384,384]{1,0:T(8,128)(2,1)S(1)}, bf16[384,384]{1,0:T(8,128)(2,1)}, u32[]{:S(2)}) copy-start(bf16[384,384]{1,0:T(8,128)(2,1)} %param.10) | copy-start | bytes 884740
  7.2 3.7 copy-start.20
  7.2 7.0 %copy-start.24 = (s32[1,1,8]{2,1,0:T(1,128)S(1)}, s32[1,1,8]{2,1,0:T(1,128)}, u32[]{:S(2)}) copy-start(s32[1,1,8]{2,1,0:T(1,128)} %param.12) | copy-start | bytes 100
  7.2 174.2 %all-gather.3.cloned.1.call-start = ((), (), s32[]{:S(2)}) async-start(), calls=%async_computation | async-start | bytes 26738688 | tf_op jit(solution)/shard_map/all_gather | solution.py:104
  10.9 380.8 %all-reduce.5.cloned.1.call-start = ((), (), s32[]{:S(2)}) async-start(), calls=%async_computation.1 | async-start | bytes 11796480 | tf_op jit(solution)/shard_map/psum | solution.py:133
  11.5 7.3 %collective-permute-start.1 = (bf16[1,32,384]{2,1,0:T(8,128)(2,1)}, bf16[1,32,384]{2,1,0:T(8,128)(2,1)S(1)}, u32[]{:S(2)}, u32[]{:S(2)}) collective-permute-start(bf16[1,32,384]{2,1,0:T(8,128)(2,1)} %get-tuple-element.22), channel_id=1, source_target_pairs={{8,0},{16,8},{24,16},{32,24},{40,32},{48,40},{56,48},{64,56},{72,6... | collective-permute-start | bytes 73736 | tf_op jit(solution)/shard_map/ppermute | solution.py:21
  13.0 5.6 %collective-permute-start = (bf16[1,32,384]{2,1,0:T(8,128)(2,1)S(1)}, bf16[1,32,384]{2,1,0:T(8,128)(2,1)S(1)}, u32[]{:S(2)}, u32[]{:S(2)}) collective-permute-start(bf16[1,32,384]{2,1,0:T(8,128)(2,1)S(1)} %get-tuple-element.23), channel_id=1, source_target_pairs={{0,8},{8,16},{16,24},{24,32},{32,40},{40,48},{48,56},{56,64},{64,7... | collective-permute-start | bytes 73736 | tf_op jit(solution)/shard_map/ppermute | solution.py:19
  19.1 5.9 %collective-permute-start.2 = (bf16[66,1,384]{2,1,0:T(2,128)(2,1)S(1)}, bf16[66,1,384]{2,1,0:T(2,128)(2,1)S(1)}, u32[]{:S(2)}, u32[]{:S(2)}) collective-permute-start(bf16[66,1,384]{2,1,0:T(2,128)(2,1)S(1)} %get-tuple-element.20), channel_id=1, source_target_pairs={{0,1},{1,2},{2,3},{3,4},{4,5},{5,6},{6,7},{8,9},{9,10},{10,11},{11... | collective-permute-start | bytes 152072 | tf_op jit(solution)/shard_map/ppermute | solution.py:19
  22.6 5.6 %collective-permute-start.3 = (bf16[66,1,384]{2,1,0:T(2,128)(2,1)S(1)}, bf16[66,1,384]{2,1,0:T(2,128)(2,1)S(1)}, u32[]{:S(2)}, u32[]{:S(2)}) collective-permute-start(bf16[66,1,384]{2,1,0:T(2,128)(2,1)S(1)} %get-tuple-element.21), channel_id=1, source_target_pairs={{1,0},{2,1},{3,2},{4,3},{5,4},{6,5},{7,6},{9,8},{10,9},{11,10},{12... | collective-permute-start | bytes 152072 | tf_op jit(solution)/shard_map/ppermute | solution.py:21
  34.4 2.6 copy-start.1
  34.4 2.6 copy-start.3
  34.4 5.2 copy-start.5
  34.4 6.3 %copy-start.7 = (bf16[1,64,32,384]{3,2,1,0:T(8,128)(2,1)}, bf16[1,64,32,384]{3,2,1,0:T(8,128)(2,1)S(1)}, u32[]{:S(2)}) copy-start(bf16[1,64,32,384]{3,2,1,0:T(8,128)(2,1)S(1)} %get-tuple-element.15) | copy-start | bytes 4718596
  34.4 7.4 %copy-start.9 = (bf16[1,64,32,384]{3,2,1,0:T(8,128)(2,1)}, bf16[1,64,32,384]{3,2,1,0:T(8,128)(2,1)S(1)}, u32[]{:S(2)}) copy-start(bf16[1,64,32,384]{3,2,1,0:T(8,128)(2,1)S(1)} %get-tuple-element.16) | copy-start | bytes 4718596
  34.4 8.5 %copy-start.11 = (bf16[1,64,32,384]{3,2,1,0:T(8,128)(2,1)}, bf16[1,64,32,384]{3,2,1,0:T(8,128)(2,1)S(1)}, u32[]{:S(2)}) copy-start(bf16[1,64,32,384]{3,2,1,0:T(8,128)(2,1)S(1)} %get-tuple-element.17) | copy-start | bytes 4718596
  34.4 9.6 %copy-start.13 = (bf16[1,64,32,384]{3,2,1,0:T(8,128)(2,1)}, bf16[1,64,32,384]{3,2,1,0:T(8,128)(2,1)S(1)}, u32[]{:S(2)}) copy-start(bf16[1,64,32,384]{3,2,1,0:T(8,128)(2,1)S(1)} %get-tuple-element.18) | copy-start | bytes 4718596
  34.5 4.0 copy-start.19
  44.1 1.4 copy-start.15
  46.6 134.8 %copy-start.23 = (f32[1,1,16]{2,1,0:T(1,128)S(1)}, f32[1,1,16]{2,1,0:T(1,128)}, u32[]{:S(2)}) copy-start(f32[1,1,16]{2,1,0:T(1,128)} %param.15) | copy-start | bytes 196
  213.4 1.9 copy-start.18
  213.4 2.3 copy-start.21
  220.8 1.8 copy-start.16
  222.6 1.8 copy-start.14
  224.4 1.8 copy-start.12
  226.3 1.8 copy-start.10
  228.1 1.8 copy-start.8
  229.9 1.8 copy-start.6
  231.8 1.8 copy-start.4
  233.6 1.8 copy-start.2
  235.4 1.8 copy-start.17
  239.1 295.0 %all-reduce.7.cloned.1.call-start = ((), (), s32[]{:S(2)}) async-start(), calls=%async_computation.2 | async-start | bytes 11796480 | tf_op jit(solution)/shard_map/psum | solution.py:133
  534.1 5.3 copy-start.22
Sparse Core Ops, SparseCore 0:
  11.0 170.3 all-gather.2
  239.2 152.3 all-reduce.4
  394.4 139.6 all-reduce.6
